TPU v7x, 512 devices: a whole 4x8x8 slice. The times are simulated.
512 devices in a mesh: lat: 32 (over z, y_hi, core), lon: 16 (over y_lo, x).
Axes of the slice: x: 4, y: 8 (y_hi: 2, y_lo: 4; y = y_hi * 4 + y_lo), z: 8, core: 2. Of those that a mesh axis runs over, the one named last changes fastest.
Arguments:
- fields: float32 [5, 32, 32, 4096], P(None, None, 'lat', 'lon'), may hold values from -6 to 6
- east_courant: float32 [32, 32, 4096], P(None, 'lat', 'lon'), may hold values from -0.45 to 0.45
- north_courant: float32 [32, 32, 4096], P(None, 'lat', 'lon'), may hold values from -0.45 to 0.45
- offsets: int32 [32], P('lat'), may hold values from -8 to 7
- lower_blocks: float32 [5, 5, 31, 32], P(None, None, None, 'lat'), may hold values from -0.4 to 0.4
- pivot_inverse: float32 [5, 5, 32, 32], P(None, None, None, 'lat'), may hold values from -0.36 to 1, as said below
- upper_blocks: float32 [5, 5, 31, 32], P(None, None, None, 'lat'), may hold values from -0.4 to 0.4
Outputs:
- solved: float32 [5, 32, 32, 4096], P(None, None, 'lat', 'lon')
Inputs may be any that keep to these rules, and one draw needn't show every extreme that they name: `pivot_inverse`: diagonal entries of each 5 x 5 block lie between 0.3 and 1; off-diagonal entries are at most 0.36 in magnitude.
All inputs are finite; a program needn't handle non-finite values.
Results may differ from a plain program's by a relative error of at most 0.0001.
Values sent between devices are 32-bit elements; how exact they have to be, the bound alone decides.
A program may use at most 64 MiB of HBM per device.

v0:
```python
import jax
import jax.numpy as jnp
from jax import lax
from jax.sharding import PartitionSpec as P


def padded(block, sides, width, periodic):
    for axis, dim in sides:
        count = lax.axis_size(axis)
        forward = [(i, i + 1) for i in range(count - 1)]
        if periodic:
            forward.append((count - 1, 0))
        backward = [(target, source) for source, target in forward]
        low = lax.ppermute(
            lax.slice_in_dim(block, block.shape[dim] - width, None, axis=dim), axis, forward
        )
        high = lax.ppermute(lax.slice_in_dim(block, 0, width, axis=dim), axis, backward)
        block = jnp.concatenate([low, block, high], axis=dim)
    return block


def apply_block(block, vector):
    return jnp.einsum("abj,bji->aji", block, vector, precision=lax.Precision.HIGHEST)


def column_solve(advected, lower_blocks, pivot_inverse, upper_blocks):
    first = apply_block(pivot_inverse[:, :, 0], advected[:, 0])

    def forward_step(previous, inputs):
        right, lower, pivot = inputs
        current = apply_block(pivot, right - apply_block(lower, previous))
        return (current, current)

    inputs = (
        jnp.moveaxis(advected[:, 1:], 1, 0),
        jnp.moveaxis(lower_blocks, 2, 0),
        jnp.moveaxis(pivot_inverse[:, :, 1:], 2, 0),
    )
    last, rest = lax.scan(forward_step, first, inputs)
    forward = jnp.concatenate([first[None], rest], axis=0)

    def backward_step(following, inputs):
        current_forward, upper = inputs
        current = current_forward - apply_block(upper, following)
        return (current, current)

    top, lower_rest = lax.scan(
        backward_step, last, (forward[:-1], jnp.moveaxis(upper_blocks, 2, 0)), reverse=True
    )
    solved = jnp.concatenate([lower_rest, last[None]], axis=0)
    return jnp.moveaxis(solved, 0, 1)


def body(fields, east_courant, north_courant, offsets, lower_blocks, pivot_inverse, upper_blocks):
    cycle_count = lax.axis_size("lon")
    cycle_place = lax.axis_index("lon")
    band_place = lax.axis_index("lat")
    row_count = fields.shape[2]
    width = fields.shape[3]
    field_count = fields.shape[0]
    displace = jnp.mod(offsets, cycle_count)
    wanted = jnp.mod(cycle_place - displace, cycle_count)
    piece = lax.all_gather(fields, "lon", axis=3, tiled=True)
    span = piece.shape[3]
    begin = wanted * width
    valid = (begin >= 0) & (begin <= span - width)
    safe = jnp.clip(begin, 0, span - width)

    def one_row(block, anchor):
        return lax.dynamic_slice_in_dim(block, anchor, width, 2)

    taken = jax.vmap(one_row, in_axes=(2, 0), out_axes=2)(piece, safe)
    moved = jnp.where(valid[None, None, :, None], taken, 0.0)
    global_rows = band_place * row_count + jnp.arange(row_count, dtype=jnp.int32)
    total_rows = row_count * lax.axis_size("lat")
    north_wall = jnp.where((global_rows == total_rows - 1)[None, :, None], 0.0, north_courant)
    lat_stack = jnp.concatenate([moved, north_wall[None]], axis=0)
    lon_stack = jnp.concatenate([moved, east_courant[None]], axis=0)
    lat_padded = padded(lat_stack, (("lat", 2),), 1, False)
    lon_padded = padded(lon_stack, (("lon", 3),), 1, True)
    east_flux = (
        jnp.maximum(east_courant, 0.0) * moved
        + jnp.minimum(east_courant, 0.0) * lon_padded[:field_count, :, :, 2:]
    )
    west_courant = lon_padded[field_count, :, :, :-2]
    west_flux = (
        jnp.maximum(west_courant, 0.0) * lon_padded[:field_count, :, :, :-2]
        + jnp.minimum(west_courant, 0.0) * moved
    )
    north_flux = (
        jnp.maximum(north_wall, 0.0) * moved
        + jnp.minimum(north_wall, 0.0) * lat_padded[:field_count, :, 2:, :]
    )
    south_courant = lat_padded[field_count, :, :-2, :]
    south_flux = (
        jnp.maximum(south_courant, 0.0) * lat_padded[:field_count, :, :-2, :]
        + jnp.minimum(south_courant, 0.0) * moved
    )
    advected = moved - (east_flux - west_flux) - (north_flux - south_flux)
    return column_solve(advected, lower_blocks, pivot_inverse, upper_blocks)


def solution(mesh):
    in_specs = (
        P(None, None, "lat", "lon"),
        P(None, "lat", "lon"),
        P(None, "lat", "lon"),
        P("lat"),
        P(None, None, None, "lat"),
        P(None, None, None, "lat"),
        P(None, None, None, "lat"),
    )
    out_specs = P(None, None, "lat", "lon")
    return jax.shard_map(body, mesh=mesh, in_specs=in_specs, out_specs=out_specs, check_vma=False)
```

profile of v0, /device:TPU:62, one launch (start us, length us, event | category | flops | bytes accessed | tf_op | source)
XLA Modules:
  0.0 152.5 jit_solution(4412390770514833927)
XLA Ops:
  6.5 1.7 %copy.14 = f32[5,32,1,256]{3,0,2,1:T(8,128)} copy(f32[5,32,1,256]{3,2,1,0:T(1,128)} %param.11) | data formatting | bytes 327680 | tf_op args[0]
  9.0 0.8 slice.53
  9.8 0.8 copy.31
  10.7 0.1 copy.17
  10.8 0.9 copy.16
  11.7 0.9 copy.18
  12.5 0.8 broadcast_maximum_fusion.2
  13.3 0.8 broadcast_maximum_fusion.1
  14.2 88.7 %all-gather.2.cloned.1.call-done = f32[5,32,1,4096]{3,0,2,1:T(8,128)} async-done(((f32[5,32,1,256]{3,0,2,1:T(8,128)}), f32[5,32,1,4096]{3,0,2,1:T(8,128)}) %all-gather.2.cloned.1.call-update) | async-done | bytes 2621456 | tf_op jit(solution)/shard_map/all_gather | solution.py:63
  102.9 1.1 dynamic-slice_select_fusion
  104.1 0.9 fusion.25
  104.9 4.4 %collective-permute-start.1 = (f32[6,32,1,1]{3,0,2,1:T(8,128)S(1)}, f32[6,32,1,1]{3,0,2,1:T(8,128)S(1)}, u32[]{:S(2)}, u32[]{:S(2)}) collective-permute-start(f32[6,32,1,1]{3,0,2,1:T(8,128)S(1)} %get-tuple-element.182), channel_id=1, source_target_pairs={{0,1},{1,2},{2,3},{3,4},{4,5},{5,6},{6,7},{7,8},{8,9},{9,10},{10,1... | collective-permute-start | bytes 2312 | tf_op jit(solution)/shard_map/ppermute | solution.py:14
  109.4 1.9 %collective-permute-start.3 = (f32[6,32,1,256]{3,0,2,1:T(8,128)S(1)}, f32[6,32,1,256]{3,0,2,1:T(8,128)S(1)}, u32[]{:S(2)}, u32[]{:S(2)}) collective-permute-start(f32[6,32,1,256]{3,0,2,1:T(8,128)S(1)} %pad_maximum_fusion.4), channel_id=1, source_target_pairs={{0,16},{16,32},{32,48},{48,64},{64,80},{80,96},{96,112},{112,128},... | collective-permute-start | bytes 589832 | tf_op jit(solution)/shard_map/ppermute | solution.py:14
  111.3 7.5 %collective-permute-start.2 = (f32[6,32,1,256]{3,0,2,1:T(8,128)S(1)}, f32[6,32,1,256]{3,0,2,1:T(8,128)S(1)}, u32[]{:S(2)}, u32[]{:S(2)}) collective-permute-start(f32[6,32,1,256]{3,0,2,1:T(8,128)S(1)} %pad_maximum_fusion.4), channel_id=1, source_target_pairs={{16,0},{32,16},{48,32},{64,48},{80,64},{96,80},{112,96},{128,112},... | collective-permute-start | bytes 589832 | tf_op jit(solution)/shard_map/ppermute | solution.py:17
  118.9 1.9 %collective-permute-start = (f32[6,32,1,1]{3,0,2,1:T(8,128)S(1)}, f32[6,32,1,1]{3,0,2,1:T(8,128)S(1)}, u32[]{:S(2)}, u32[]{:S(2)}) collective-permute-start(f32[6,32,1,1]{3,0,2,1:T(8,128)S(1)} %get-tuple-element.181), channel_id=1, source_target_pairs={{1,0},{2,1},{3,2},{4,3},{5,4},{6,5},{7,6},{8,7},{9,8},{10,9},{11,1... | collective-permute-start | bytes 2312 | tf_op jit(solution)/shard_map/ppermute | solution.py:17
  120.8 1.0 broadcast_maximum_fusion
  121.8 0.8 collective-permute-done.3
  122.7 6.9 %collective-permute-done = f32[6,32,1,1]{3,0,2,1:T(8,128)S(1)} collective-permute-done((f32[6,32,1,1]{3,0,2,1:T(8,128)S(1)}, f32[6,32,1,1]{3,0,2,1:T(8,128)S(1)}, u32[]{:S(2)}, u32[]{:S(2)}) %collective-permute-start) | collective-permute-done | bytes 800 | tf_op jit(solution)/shard_map/ppermute | solution.py:17
  129.6 0.4 fusion.17
  130.2 8.8 %while.29 = (s32[]{:T(128)}, f32[5,1,256]{2,0,1:T(8,128)S(1)}, f32[31,5,1,256]{3,1,2,0:T(8,128)S(1)}, f32[31,5,1,256]{3,1,2,0:T(8,128)S(1)}, f32[31,5,5,1]{2,1,3...) while((s32[]{:T(128)}, f32[5,1,256]{2,0,1:T(8,128)S(1)}, f32[31,5,1,256]{3,1,2,0:T(8,128)S(1)}, ...), condition=%wide.region_1.2_spmd, body=%wide.region_0.1_spmd.sunk | while | flops 154882 | bytes 56397 | solution.py:39
  130.5 0.1 fusion.40
  130.8 0.1 fusion.40
  131.1 0.1 fusion.40
  131.3 0.1 fusion.40
  131.6 0.1 fusion.40
  131.9 0.1 fusion.40
  132.2 0.1 fusion.40
  132.5 0.1 fusion.40
  132.8 0.1 fusion.40
  133.0 0.1 fusion.40
  133.3 0.1 fusion.40
  133.6 0.1 fusion.40
  133.9 0.1 fusion.40
  134.2 0.1 fusion.40
  134.5 0.1 fusion.40
  134.7 0.1 fusion.40
  135.0 0.1 fusion.40
  135.3 0.1 fusion.40
  135.6 0.1 fusion.40
  135.9 0.1 fusion.40
  136.2 0.1 fusion.40
  136.4 0.1 fusion.40
  136.7 0.1 fusion.40
  137.0 0.1 fusion.40
  138.4 0.1 fusion.40
  138.7 0.1 fusion.40
  139.1 5.7 %while.30 = (s32[]{:T(128)}, f32[5,1,256]{2,0,1:T(8,128)S(1)}, f32[31,5,1,256]{3,2,0,1:T(1,128)S(1)}, f32[31,5,1,256]{3,1,2,0:T(8,128)S(1)}, f32[31,5,5,1]{2,1,3,0:T(8,128)S(1)}, /*index=5*/s32[]{:T(128)}, s32[]{:T(128)}) while((s32[]{:T(128)}, f32[5,1,256]{2,0,1:T(8,128)S(1)}, f32[31,5,1,256]{3,2,0,1:T(1,128)S(1)}, ...), condition=%wide.region_3.4_spmd, body=%wide.region_2.3_spmd.sunk | while | flops 78083 | bytes 50269 | solution.py:47
  144.8 0.8 maximum_bitcast_fusion
  (149 shorter events, 10.3 us)
Async XLA Ops:
  6.5 123.1 %copy-start = (f32[32,1,256]{2,1,0:T(1,128)S(1)}, f32[32,1,256]{2,1,0:T(1,128)}, u32[]{:S(2)}) copy-start(f32[32,1,256]{2,1,0:T(1,128)} %param.12) | copy-start | bytes 98308
  6.5 96.4 %all-gather.2.cloned.1.call-start = ((), (), s32[]{:S(2)}) async-start(), calls=%async_computation | async-start | bytes 4456448 | tf_op jit(solution)/shard_map/all_gather | solution.py:63
  104.9 15.8 %collective-permute-start.1 = (f32[6,32,1,1]{3,0,2,1:T(8,128)S(1)}, f32[6,32,1,1]{3,0,2,1:T(8,128)S(1)}, u32[]{:S(2)}, u32[]{:S(2)}) collective-permute-start(f32[6,32,1,1]{3,0,2,1:T(8,128)S(1)} %get-tuple-element.182), channel_id=1, source_target_pairs={{0,1},{1,2},{2,3},{3,4},{4,5},{5,6},{6,7},{7,8},{8,9},{9,10},{10,1... | collective-permute-start | bytes 2312 | tf_op jit(solution)/shard_map/ppermute | solution.py:14
  109.4 13.3 %collective-permute-start.3 = (f32[6,32,1,256]{3,0,2,1:T(8,128)S(1)}, f32[6,32,1,256]{3,0,2,1:T(8,128)S(1)}, u32[]{:S(2)}, u32[]{:S(2)}) collective-permute-start(f32[6,32,1,256]{3,0,2,1:T(8,128)S(1)} %pad_maximum_fusion.4), channel_id=1, source_target_pairs={{0,16},{16,32},{32,48},{48,64},{64,80},{80,96},{96,112},{112,128},... | collective-permute-start | bytes 589832 | tf_op jit(solution)/shard_map/ppermute | solution.py:14
  111.3 18.3 %collective-permute-start.2 = (f32[6,32,1,256]{3,0,2,1:T(8,128)S(1)}, f32[6,32,1,256]{3,0,2,1:T(8,128)S(1)}, u32[]{:S(2)}, u32[]{:S(2)}) collective-permute-start(f32[6,32,1,256]{3,0,2,1:T(8,128)S(1)} %pad_maximum_fusion.4), channel_id=1, source_target_pairs={{16,0},{32,16},{48,32},{64,48},{80,64},{96,80},{112,96},{128,112},... | collective-permute-start | bytes 589832 | tf_op jit(solution)/shard_map/ppermute | solution.py:17
  118.9 10.8 %collective-permute-start = (f32[6,32,1,1]{3,0,2,1:T(8,128)S(1)}, f32[6,32,1,1]{3,0,2,1:T(8,128)S(1)}, u32[]{:S(2)}, u32[]{:S(2)}) collective-permute-start(f32[6,32,1,1]{3,0,2,1:T(8,128)S(1)} %get-tuple-element.181), channel_id=1, source_target_pairs={{1,0},{2,1},{3,2},{4,3},{5,4},{6,5},{7,6},{8,7},{9,8},{10,9},{11,1... | collective-permute-start | bytes 2312 | tf_op jit(solution)/shard_map/ppermute | solution.py:17
Sparse Core Ops, SparseCore 0:
  9.4 93.4 all-gather.1
where the time goes:
time: 153 us; the launch traced here: 152 us
  waiting for transfers between devices  96.5 us (63%)
  starting transfers between devices  15.8 us (10%)
  between operations  14.3 us (9%)
  matrix products  13.1 us (9%)
  other arithmetic  6.02 us (4%)
  local copies, waits for them, and re-layouts  5.95 us (4%)
    all_gather x1, waiting for transfers between devices, body(): piece = lax.all_gather(fields, 'lon', axis=3, tiled=True)  88.7 us
    dot_general x94, matrix products, apply_block(): jnp.einsum('abj,bji->aji', block, vector, precision=lax.Precision.HIGHEST)  13.1 us
    ppermute x2, starting transfers between devices, padded(): lax.ppermute(lax.slice_in_dim(block, 0, width, axis=dim), axis, backward)  9.47 us
    ppermute x2, waiting for transfers between devices, padded(): lax.ppermute(lax.slice_in_dim(block, 0, width, axis=dim), axis, backward)  6.91 us
    ppermute x2, starting transfers between devices, padded(): lax.ppermute(lax.slice_in_dim(block, block.shape[dim] - width, None, axis...  6.28 us
    unnamed x11, local copies, waits for them, and re-layouts  4.32 us
  transfers between devices with their start and end apart: 5, of which 3 were waited for; matrix products, arithmetic and copies ran while one was open for 4% of the time, Pallas kernels for 0%

commit v1 on v0

--- a/solution.py
+++ b/solution.py
@@ -60,7 +60,9 @@
     field_count = fields.shape[0]
     displace = jnp.mod(offsets, cycle_count)
     wanted = jnp.mod(cycle_place - displace, cycle_count)
-    piece = lax.all_gather(fields, "lon", axis=3, tiled=True)
+    piece = jnp.concatenate(
+        lax.all_to_all(jnp.stack([fields] * lax.axis_size("lon")), "lon", 0, 0), axis=3
+    )
     span = piece.shape[3]
     begin = wanted * width
     valid = (begin >= 0) & (begin <= span - width)

time: 153 us -> 117 us (0.76)
  the two profiles are of different devices: /device:TPU:62 before, /device:TPU:235 now
where the time goes in v1:
time: 117 us; the launch traced here: 116 us
  waiting for transfers between devices  65.4 us (56%)
  starting transfers between devices  24.5 us (21%)
  matrix products  12.5 us (11%)
  local copies, waits for them, and re-layouts  10.3 us (9%)
  other arithmetic  1.36 us (1%)
  loops' own time  1.17 us (1%)
    all_to_all x1, waiting for transfers between devices, body(): lax.all_to_all(jnp.stack([fields] * lax.axis_size('lon')), 'lon', 0, 0)  54.3 us
    ppermute x2, starting transfers between devices, padded(): lax.ppermute(lax.slice_in_dim(block, block.shape[dim] - width, None, axis...  15.1 us
    dot_general x94, matrix products, apply_block(): jnp.einsum('abj,bji->aji', block, vector, precision=lax.Precision.HIGHEST)  12.5 us
    ppermute x2, waiting for transfers between devices, padded(): lax.ppermute(lax.slice_in_dim(block, 0, width, axis=dim), axis, backward)  6.68 us
    all_to_all x1, starting transfers between devices, body(): lax.all_to_all(jnp.stack([fields] * lax.axis_size('lon')), 'lon', 0, 0)  5.56 us
    ppermute x2, waiting for transfers between devices, padded(): lax.ppermute(lax.slice_in_dim(block, block.shape[dim] - width, None, axis...  4.47 us
    ppermute x2, starting transfers between devices, padded(): lax.ppermute(lax.slice_in_dim(block, 0, width, axis=dim), axis, backward)  3.84 us
    reshape x1, local copies, waits for them, and re-layouts, body(): jnp.concatenate(lax.all_to_all(jnp.stack([fields] * lax.axis_size('lon'))...  2.99 us
  transfers between devices with their start and end apart: 5, of which 3 were waited for; matrix products, arithmetic and copies ran while one was open for 1% of the time, Pallas kernels for 0%

profile of v1, /device:TPU:235, one launch (start us, length us, event | category | flops | bytes accessed | tf_op | source)
XLA Modules:
  0.0 116.3 jit_solution(6270621349394675919)
XLA Ops:
  0.0 0.9 copy.61
  0.9 1.8 %stack.2 = f32[16,5,32,1,256]{4,2,1,3,0:T(8,128)} broadcast(f32[5,32,256]{2,1,0:T(8,128)S(1)} %bitcast.137), dimensions={1,2,4} | broadcast | bytes 2785280 | tf_op jit(solution)/shard_map/stack | solution.py:64
  2.8 5.6 %all-to-all-start = ((f32[16,5,32,1,256]{4,2,1,3,0:T(8,128)}), f32[16,5,32,1,256]{4,2,1,3,0:T(8,128)S(1)}, u32[]{:S(2)}, u32[]{:S(2)}) async-start(f32[16,5,32,1,256]{4,2,1,3,0:T(8,128)} %stack.2), calls=%async_computation | async-start | bytes 5242880 | tf_op jit(solution)/shard_map/all_to_all | solution.py:64
  9.3 0.2 copy.29
  9.4 0.2 copy.30
  9.6 0.1 copy.32
  9.8 54.3 %all-to-all-done = f32[16,5,32,1,256]{4,2,1,3,0:T(8,128)S(1)} async-done(((f32[16,5,32,1,256]{4,2,1,3,0:T(8,128)}), f32[16,5,32,1,256]{4,2,1,3,0:T(8,128)S(1)}, u32[]{:S(2)}, u32[]{:S(2)}) %all-to-all-start) | async-done | bytes 2621472 | tf_op jit(solution)/shard_map/all_to_all | solution.py:64
  64.1 3.0 %copy.24 = f32[5,32,1,16,256]{4,3,1,0,2:T(8,128)} copy(f32[5,32,1,16,256]{4,1,0,2,3:T(8,128)S(1)} %bitcast.134) | data formatting | bytes 5242880 | tf_op jit(solution)/shard_map/reshape | solution.py:63
  67.1 2.6 %transpose_reshape.3 = f32[1,5,32,4096]{3,2,1,0:T(8,128)S(1)} reshape(f32[5,32,1,16,256]{4,3,1,0,2:T(8,128)} %copy.24) | data formatting | bytes 5242880 | tf_op jit(solution)/shard_map/vmap()/transpose;reshape | solution.py:72
  69.9 6.1 %collective-permute-start.1 = (f32[6,32,1,1]{3,1,0,2:T(8,128)S(1)}, f32[6,32,1,1]{3,1,0,2:T(8,128)S(1)}, u32[]{:S(2)}, u32[]{:S(2)}) collective-permute-start(f32[6,32,1,1]{3,1,0,2:T(8,128)S(1)} %get-tuple-element.196), channel_id=1, source_target_pairs={{0,1},{1,2},{2,3},{3,4},{4,5},{5,6},{6,7},{7,8},{8,9},{9,10},{10,1... | collective-permute-start | bytes 2312 | tf_op jit(solution)/shard_map/ppermute | solution.py:14
  76.0 9.1 %collective-permute-start.3 = (f32[6,32,1,256]{3,1,0,2:T(8,128)S(1)}, f32[6,32,1,256]{3,1,0,2:T(8,128)S(1)}, u32[]{:S(2)}, u32[]{:S(2)}) collective-permute-start(f32[6,32,1,256]{3,1,0,2:T(8,128)S(1)} %pad_maximum_fusion.1), channel_id=1, source_target_pairs={{0,16},{16,32},{32,48},{48,64},{64,80},{80,96},{96,112},{112,128},... | collective-permute-start | bytes 589832 | tf_op jit(solution)/shard_map/ppermute | solution.py:14
  85.1 1.9 %collective-permute-start.2 = (f32[6,32,1,256]{3,1,0,2:T(8,128)S(1)}, f32[6,32,1,256]{3,1,0,2:T(8,128)S(1)}, u32[]{:S(2)}, u32[]{:S(2)}) collective-permute-start(f32[6,32,1,256]{3,1,0,2:T(8,128)S(1)} %pad_maximum_fusion.1), channel_id=1, source_target_pairs={{16,0},{32,16},{48,32},{64,48},{80,64},{96,80},{112,96},{128,112},... | collective-permute-start | bytes 589832 | tf_op jit(solution)/shard_map/ppermute | solution.py:17
  87.0 1.9 %collective-permute-start = (f32[6,32,1,1]{3,1,0,2:T(8,128)S(1)}, f32[6,32,1,1]{3,1,0,2:T(8,128)S(1)}, u32[]{:S(2)}, u32[]{:S(2)}) collective-permute-start(f32[6,32,1,1]{3,1,0,2:T(8,128)S(1)} %get-tuple-element.195), channel_id=1, source_target_pairs={{1,0},{2,1},{3,2},{4,3},{5,4},{6,5},{7,6},{8,7},{9,8},{10,9},{11,1... | collective-permute-start | bytes 2312 | tf_op jit(solution)/shard_map/ppermute | solution.py:17
  89.0 4.5 %collective-permute-done.3 = f32[6,32,1,256]{3,1,0,2:T(8,128)S(1)} collective-permute-done((f32[6,32,1,256]{3,1,0,2:T(8,128)S(1)}, f32[6,32,1,256]{3,1,0,2:T(8,128)S(1)}, u32[]{:S(2)}, u32[]{:S(2)}) %collective-permute-start.3) | collective-permute-done | bytes 196640 | tf_op jit(solution)/shard_map/ppermute | solution.py:14
  93.5 6.7 %collective-permute-done.2 = f32[6,32,1,256]{3,1,0,2:T(8,128)S(1)} collective-permute-done((f32[6,32,1,256]{3,1,0,2:T(8,128)S(1)}, f32[6,32,1,256]{3,1,0,2:T(8,128)S(1)}, u32[]{:S(2)}, u32[]{:S(2)}) %collective-permute-start.2) | collective-permute-done | bytes 196640 | tf_op jit(solution)/shard_map/ppermute | solution.py:17
  100.2 0.2 fusion.17
  100.6 9.2 %while.29 = (s32[]{:T(128)}, f32[5,1,256]{2,0,1:T(8,128)S(1)}, f32[31,5,1,256]{3,1,2,0:T(8,128)S(1)}, f32[31,5,1,256]{3,0,1,2:T(8,128)S(1)}, f32[31,5,5,1]{2,1,3...) while((s32[]{:T(128)}, f32[5,1,256]{2,0,1:T(8,128)S(1)}, f32[31,5,1,256]{3,1,2,0:T(8,128)S(1)}, ...), condition=%wide.region_1.2_spmd, body=%wide.region_0.1_spmd.sunk | while | flops 154882 | bytes 62557 | solution.py:39
  100.6 0.1 fusion.43
  100.9 0.1 fusion.43
  101.2 0.1 fusion.43
  101.5 0.1 fusion.43
  101.8 0.1 fusion.43
  102.1 0.1 fusion.43
  102.4 0.1 fusion.43
  102.7 0.1 fusion.43
  103.0 0.1 fusion.43
  103.2 0.1 fusion.43
  103.5 0.1 fusion.43
  103.8 0.1 fusion.43
  104.1 0.1 fusion.43
  104.4 0.1 fusion.43
  104.7 0.1 fusion.43
  105.0 0.1 fusion.43
  105.3 0.1 fusion.43
  105.6 0.1 fusion.43
  105.9 0.1 fusion.43
  106.2 0.1 fusion.43
  106.5 0.1 fusion.43
  106.8 0.1 fusion.43
  107.1 0.1 fusion.43
  107.4 0.1 fusion.43
  107.7 0.1 fusion.43
  108.0 0.1 fusion.43
  108.3 0.1 fusion.43
  108.6 0.1 fusion.43
  109.4 0.1 fusion.43
  109.9 5.6 %while.30 = (s32[]{:T(128)}, f32[5,1,256]{2,0,1:T(8,128)S(1)}, f32[31,5,1,256]{3,2,0,1:T(1,128)S(1)}, f32[31,5,1,256]{3,1,2,0:T(8,128)S(1)}, f32[31,5,5,1]{2,1,3,0:T(8,128)S(1)}, /*index=5*/s32[]{:T(128)}, s32[]{:T(128)}) while((s32[]{:T(128)}, f32[5,1,256]{2,0,1:T(8,128)S(1)}, f32[31,5,1,256]{3,2,0,1:T(1,128)S(1)}, ...), condition=%wide.region_3.4_spmd, body=%wide.region_2.3_spmd.sunk | while | flops 78083 | bytes 50277 | solution.py:47
  115.5 0.8 maximum_bitcast_fusion
  (187 shorter events, 10.5 us)
Async XLA Ops:
  2.8 6.3 %copy-start = (f32[5,5,32,1]{2,3,1,0:T(1,128)S(1)}, f32[5,5,32,1]{2,3,1,0:T(1,128)}, u32[]{:S(2)}) copy-start(f32[5,5,32,1]{2,3,1,0:T(1,128)} %param.16) | copy-start | bytes 9604
  2.8 6.5 %copy-start.3 = (f32[5,5,31,1]{2,3,1,0:T(1,128)S(1)}, f32[5,5,31,1]{2,3,1,0:T(1,128)}, u32[]{:S(2)}) copy-start(f32[5,5,31,1]{2,3,1,0:T(1,128)} %param.15) | copy-start | bytes 9304
  2.8 6.8 %copy-start.4 = (f32[5,5,31,1]{2,3,1,0:T(1,128)S(1)}, f32[5,5,31,1]{2,3,1,0:T(1,128)}, u32[]{:S(2)}) copy-start(f32[5,5,31,1]{2,3,1,0:T(1,128)} %param.17) | copy-start | bytes 9304
  2.8 7.0 %copy-start.1 = (f32[32,1,256]{2,1,0:T(1,128)S(1)}, f32[32,1,256]{2,1,0:T(1,128)}, u32[]{:S(2)}) copy-start(f32[32,1,256]{2,1,0:T(1,128)} %param.12) | copy-start | bytes 98308
  2.8 7.0 %copy-start.2 = (f32[32,1,256]{2,1,0:T(1,128)S(1)}, f32[32,1,256]{2,1,0:T(1,128)}, u32[]{:S(2)}) copy-start(f32[32,1,256]{2,1,0:T(1,128)} %param.13) | copy-start | bytes 98308
  2.8 61.3 %all-to-all-start = ((f32[16,5,32,1,256]{4,2,1,3,0:T(8,128)}), f32[16,5,32,1,256]{4,2,1,3,0:T(8,128)S(1)}, u32[]{:S(2)}, u32[]{:S(2)}) async-start(f32[16,5,32,1,256]{4,2,1,3,0:T(8,128)} %stack.2), calls=%async_computation | async-start | bytes 5242880 | tf_op jit(solution)/shard_map/all_to_all | solution.py:64
  69.9 19.0 %collective-permute-start.1 = (f32[6,32,1,1]{3,1,0,2:T(8,128)S(1)}, f32[6,32,1,1]{3,1,0,2:T(8,128)S(1)}, u32[]{:S(2)}, u32[]{:S(2)}) collective-permute-start(f32[6,32,1,1]{3,1,0,2:T(8,128)S(1)} %get-tuple-element.196), channel_id=1, source_target_pairs={{0,1},{1,2},{2,3},{3,4},{4,5},{5,6},{6,7},{7,8},{8,9},{9,10},{10,1... | collective-permute-start | bytes 2312 | tf_op jit(solution)/shard_map/ppermute | solution.py:14
  76.0 17.5 %collective-permute-start.3 = (f32[6,32,1,256]{3,1,0,2:T(8,128)S(1)}, f32[6,32,1,256]{3,1,0,2:T(8,128)S(1)}, u32[]{:S(2)}, u32[]{:S(2)}) collective-permute-start(f32[6,32,1,256]{3,1,0,2:T(8,128)S(1)} %pad_maximum_fusion.1), channel_id=1, source_target_pairs={{0,16},{16,32},{32,48},{48,64},{64,80},{80,96},{96,112},{112,128},... | collective-permute-start | bytes 589832 | tf_op jit(solution)/shard_map/ppermute | solution.py:14
  85.1 15.1 %collective-permute-start.2 = (f32[6,32,1,256]{3,1,0,2:T(8,128)S(1)}, f32[6,32,1,256]{3,1,0,2:T(8,128)S(1)}, u32[]{:S(2)}, u32[]{:S(2)}) collective-permute-start(f32[6,32,1,256]{3,1,0,2:T(8,128)S(1)} %pad_maximum_fusion.1), channel_id=1, source_target_pairs={{16,0},{32,16},{48,32},{64,48},{80,64},{96,80},{112,96},{128,112},... | collective-permute-start | bytes 589832 | tf_op jit(solution)/shard_map/ppermute | solution.py:17
  87.0 6.5 %collective-permute-start = (f32[6,32,1,1]{3,1,0,2:T(8,128)S(1)}, f32[6,32,1,1]{3,1,0,2:T(8,128)S(1)}, u32[]{:S(2)}, u32[]{:S(2)}) collective-permute-start(f32[6,32,1,1]{3,1,0,2:T(8,128)S(1)} %get-tuple-element.195), channel_id=1, source_target_pairs={{1,0},{2,1},{3,2},{4,3},{5,4},{6,5},{7,6},{8,7},{9,8},{10,9},{11,1... | collective-permute-start | bytes 2312 | tf_op jit(solution)/shard_map/ppermute | solution.py:17
